TPU v7x, 768 devices: a whole 4x8x12 slice. The times are simulated.
768 devices in a mesh: dp: 24 (over z, core), ctx: 32 (over x, y).
Axes of the slice: x: 4, y: 8, z: 12, core: 2. Of those that a mesh axis runs over, the one named last changes fastest.
Arguments:
- query_heads: bfloat16 [24, 4096, 1024], P('dp', 'ctx'), may hold values from -6 to 6
- key_heads: bfloat16 [24, 4096, 1024], P('dp', 'ctx'), may hold values from -6 to 6
- value_heads: bfloat16 [24, 4096, 1024], P('dp', 'ctx'), may hold values from -6 to 6
- grad_output: bfloat16 [24, 4096, 1024], P('dp', 'ctx'), may hold values from -6 to 6
- layer_input: bfloat16 [24, 4096, 1152], P('dp', 'ctx'), may hold values from -6 to 6
Outputs:
- grad_query: bfloat16 [24, 4096, 1024], P('dp', 'ctx')
- grad_key: bfloat16 [24, 4096, 1024], P('dp', 'ctx')
- grad_value: bfloat16 [24, 4096, 1024], P('dp', 'ctx')
- grad_weight: float32 [1152, 1024], P('dp', 'ctx')
All inputs are finite; a program needn't handle non-finite values.
Results may differ from a plain program's by a relative error of at most 0.008.
Values sent between devices are 32-bit elements; how exact they have to be, the bound alone decides.
No kernel may reach another device: no remote copies, remote signals or barrier semaphores. Data moves between devices by JAX's collectives and lax.ppermute only.
A program may use at most 128 MiB of HBM per device.

v0:
```python
import math

import jax
import jax.numpy as jnp
from jax import lax
from jax.experimental import pallas as pl
from jax.experimental.pallas import tpu as pltpu
from jax.sharding import Mesh
from jax.sharding import PartitionSpec as P

HD = 128
HV = 8
DW = 1152
TOK = 128
VW = HV * HD
BF = jnp.bfloat16
F32 = jnp.float32
INTERPRET = False


def dot(a, b, ca, cb):
    if INTERPRET:
        a, b = a.astype(F32), b.astype(F32)
    return lax.dot_general(a, b, (((ca,), (cb,)), ((), ())), preferred_element_type=F32)


def call(body, outs, *args):
    return pl.pallas_call(body, out_shape=outs, interpret=INTERPRET)(*args)


def head(h):
    return slice(h * HD, (h + 1) * HD)


def states_body(q_ref, k_ref, v_ref, g_ref, st_ref):
    rows = st_ref.shape[2]
    for h in range(HV):
        s = head(h)
        for which, (a_ref, b_ref) in enumerate(((k_ref, v_ref), (q_ref, g_ref))):
            block = dot(a_ref[:, s], b_ref[:, s], 0, 0)
            if rows <= HD:
                per = HD // rows
                st_ref[h * per : (h + 1) * per, which] = block.reshape(per, rows, HD)
            else:
                st_ref[h * HD // rows, which, h * HD % rows : h * HD % rows + HD] = block


def load_state(st_ref, which, h):
    rows = st_ref.shape[2]
    if rows <= HD:
        per = HD // rows
        block = st_ref[h * per : (h + 1) * per, which].reshape(HD, HD)
    else:
        block = st_ref[h * HD // rows, which, h * HD % rows : h * HD % rows + HD]
    return block.astype(BF)


def intra_body(scale, q_ref, k_ref, v_ref, g_ref, dq_ref, dk_ref, dv_ref):
    t = lax.broadcasted_iota(jnp.int32, (TOK, TOK), 0)
    u = lax.broadcasted_iota(jnp.int32, (TOK, TOK), 1)
    causal = t >= u
    for h in range(HV):
        s = head(h)
        q, k, v, g = q_ref[:, s], k_ref[:, s], v_ref[:, s], g_ref[:, s]
        score_w = jnp.where(causal, scale * dot(q, k, 1, 1), 0.0).astype(BF)
        grad_w = jnp.where(causal, scale * dot(g, v, 1, 1), 0.0).astype(BF)
        dq_ref[:, s] = dot(grad_w, k, 1, 0)
        dk_ref[:, s] = dot(grad_w, q, 0, 0)
        dv_ref[:, s] = dot(score_w, g, 0, 0)


def scan_body(in_ref, out_ref):
    n = in_ref.shape[0]
    for which, order in enumerate((range(n), range(n)[::-1])):
        total = jnp.zeros(in_ref.shape[2:], F32)
        for i in order:
            out_ref[i, which] = total
            total = total + in_ref[i, which]


def value_body(scale, k_ref, dvi_ref, st_ref, perm_ref, dv_ref, send_ref):
    for h in range(HV):
        s = head(h)
        inter = dot(k_ref[:, s], load_state(st_ref, 1, h), 1, 0)
        dv_ref[:, s] = (dvi_ref[:, s] + scale * inter).astype(BF)
    moved = dot(dv_ref[...], perm_ref[...], 1, 0)
    wide = send_ref.shape[2]
    for m in range(send_ref.shape[0]):
        send_ref[m] = moved[:, m * wide : (m + 1) * wide]


def outer_body(scale, g_ref, v_ref, dqi_ref, dki_ref, st_ref, dq_ref, dk_ref):
    for h in range(HV):
        s = head(h)
        inter = dot(g_ref[:, s], load_state(st_ref, 0, h), 1, 1)
        dq_ref[:, s] = (dqi_ref[:, s] + scale * inter).astype(BF)
        inter = dot(v_ref[:, s], load_state(st_ref, 1, h), 1, 1)
        dk_ref[:, s] = (dki_ref[:, s] + scale * inter).astype(BF)


def pack_body(*refs):
    for i, ref in enumerate(refs[:-1]):
        refs[-1][i] = ref[...].astype(BF)


def weight_body(rscale, place_ref, dv_ref, x_ref, out_ref):
    n = dv_ref.shape[0] // 2
    total = None
    for i in range(2 * n):
        slot = 2 * lax.rem(place_ref[0] + n - i // 2, n) + lax.rem(place_ref[1] + i % 2, 2)
        part = dot(dv_ref[slot].astype(BF), x_ref[i], 0, 0)
        total = part if total is None else total + part
    total = total * rscale
    blocks, cols, _ = out_ref.shape
    for i in range(blocks):
        out_ref[i] = total[i * cols : (i + 1) * cols]


def fold_body(in_ref, out_ref):
    total = in_ref[0]
    for i in range(1, in_ref.shape[0]):
        total = total + in_ref[i]
    n = out_ref.shape[0]
    cols, rows = total.shape[0], total.shape[1] // n
    for i in range(n):
        part = total[:, i * rows : (i + 1) * rows]
        out_ref[i] = jnp.concatenate([part[j : j + 1] for j in range(cols)], axis=1)


def last_body(members, in_ref, out_ref):
    rows = out_ref.shape[1]
    cols = in_ref.shape[2] // rows
    for m in range(members):
        total = in_ref[m]
        for i in range(m + members, in_ref.shape[0], members):
            total = total + in_ref[i]
        for j in range(cols):
            at = m * cols + j
            out_ref[at : at + 1] = total[:, j * rows : (j + 1) * rows]


def on_device(sizes, query_heads, key_heads, value_heads, grad_output, layer_input):
    na, nb, nx, ny = sizes
    nc = nx * ny
    members = 2 * nb
    length = TOK * nc
    scale = 1.0 / math.sqrt(HD * length)
    rscale = 1.0 / math.sqrt(2 * na * nb * length)
    q, k, v, g = query_heads[0], key_heads[0], value_heads[0], grad_output[0]
    rows = VW // nc
    wide = VW // members
    cols = wide // nc

    def shaped(*shape, dtype=F32):
        return jax.ShapeDtypeStruct(shape, dtype)

    states = shaped(nc, 2, rows, HD)
    flat = shaped(TOK, VW)
    flat_bf = shaped(TOK, VW, dtype=BF)

    def exchange(array, axes):
        return lax.all_to_all(array, axes, 0, 0, tiled=True)

    held = exchange(call(states_body, states, q, k, v, g), ("x", "y"))

    own = layer_input[0].astype(F32)
    swap = [(0, 1), (1, 0)]
    both = [own, lax.ppermute(own, "c", swap)]
    for d in range(1, nb):
        array = lax.ppermute(own, "b", [(i, (i + d) % nb) for i in range(nb)])
        both += [array, lax.ppermute(array, "c", swap)]
    inputs = call(pack_body, shaped(members, TOK, DW, dtype=BF), *both)
    place = jnp.stack([lax.axis_index("b"), lax.axis_index("c")]).astype(jnp.int32)

    dqi, dki, dvi = call(lambda *refs: intra_body(scale, *refs), [flat] * 3, q, k, v, g)
    at = jnp.arange(VW)
    block, rest = jnp.divmod(at, VW // nc)
    member, j = jnp.divmod(rest, cols)
    perm = (at[None, :] == (member * wide + block * cols + j)[:, None]).astype(BF)

    state = exchange(call(scan_body, states, held), ("x", "y"))
    dv, send = call(
        lambda *refs: value_body(scale, *refs),
        [flat_bf, shaped(members, TOK, wide)],
        k, dvi, state, perm,
    )
    columns = exchange(send, ("b", "c"))
    dq, dk = call(lambda *refs: outer_body(scale, *refs), [flat_bf] * 2, g, v, dqi, dki, state)
    term = pl.pallas_call(
        lambda *refs: weight_body(rscale, *refs),
        in_specs=[pl.BlockSpec(memory_space=pltpu.SMEM)] + [pl.BlockSpec(memory_space=pltpu.VMEM)] * 2,
        out_shape=shaped(nc, cols, DW),
        name="weight",
        interpret=INTERPRET,
    )(place, columns, inputs)
    terms = exchange(term, ("x", "y"))
    out_rows = DW // (members * na)
    folded = call(fold_body, shaped(members * na, 1, cols * out_rows), terms)
    parts = exchange(folded, ("a", "b", "c"))
    weight = call(lambda *refs: last_body(members, *refs), shaped(members * cols, out_rows), parts)
    return dq[None], dk[None], dv[None], weight.T


def solution(mesh):
    nx, nb = SPLIT
    sizes = (mesh.shape["dp"] // 2 // nb, nb, nx, mesh.shape["ctx"] // nx)
    na, nb, nx, ny = sizes
    inner = Mesh(mesh.devices.reshape(na, nb, 2, nx, ny), ("a", "b", "c", "x", "y"))
    spec = P(("a", "b", "c"), ("x", "y"), None)

    def body(*arrays):
        return on_device(sizes, *arrays)

    return jax.shard_map(
        body,
        mesh=inner,
        in_specs=(spec,) * 5,
        out_specs=(spec, spec, spec, P(("a", "b", "c"), ("x", "y"))),
        check_vma=False,
    )


SPLIT = (4, 4)
```

profile of v0, /device:TPU:9, one launch (start us, length us, event | category | flops | bytes accessed | tf_op | source)
XLA Modules:
  0.0 220.0 jit_solution(9081198209539787781)
XLA Ops:
  0.6 2.5 %shard_map.85 = f32[32,2,32,128]{3,2,1,0:T(8,128)} custom-call(bf16[128,1024]{1,0:T(8,128)(2,1)} %bitcast.22, bf16[128,1024]{1,0:T(8,128)(2,1)} %bitcast.19, bf16[128,1024]{1,0:T(8,128)(2,1)} %bitcast.16, bf16[128,1024]{1,0:T(8,128)(2,1)} %bitcast.13), custom_call_target="tpu_custom_call" | custom-call | tf_op jit(solution)/shard_map/pallas_call | solution.py:28
  3.1 33.9 %all_to_all.25.in_ref = f32[32,2,32,128]{3,2,1,0:T(8,128)} all-to-all(f32[32,2,32,128]{3,2,1,0:T(8,128)} %shard_map.85), channel_id=1, replica_groups=mesh['a'=3,'b'=4,'c'=2,'x'=4,'y'=8] {'x','y'}, dimensions={0} | all-to-all | bytes 2097152 | tf_op jit(solution)/shard_map/all_to_all | solution.py:162
  37.0 2.3 %shard_map.86 = f32[32,2,32,128]{3,2,1,0:T(8,128)} custom-call(f32[32,2,32,128]{3,2,1,0:T(8,128)} %all_to_all.25.in_ref), custom_call_target="tpu_custom_call" | custom-call | tf_op jit(solution)/shard_map/pallas_call | solution.py:28
  39.3 5.3 %all-to-all-start.1 = ((f32[32,2,32,128]{3,2,1,0:T(8,128)}), f32[32,2,32,128]{3,2,1,0:T(8,128)S(1)}, u32[]{:S(2)}, u32[]{:S(2)}) async-start(f32[32,2,32,128]{3,2,1,0:T(8,128)} %shard_map.86), calls=%async_computation.1 | async-start | bytes 2097152 | tf_op jit(solution)/shard_map/all_to_all | solution.py:162
  44.6 4.3 %shard_map.84 = (f32[128,1024]{1,0:T(8,128)}, f32[128,1024]{1,0:T(8,128)}, f32[128,1024]{1,0:T(8,128)}) custom-call(bf16[128,1024]{1,0:T(8,128)(2,1)} %bitcast.23, bf16[128,1024]{1,0:T(8,128)(2,1)} %bitcast.20, bf16[128,1024]{1,0:T(8,128)(2,1)} %bitcast.17, bf16[128,1024]{1,0:T(8,128)(2,1)} %bitcast.14), custom_call_target="tpu_custom_call" | custom-call | tf_op jit(solution)/shard_map/pallas_call | solution.py:28
  50.6 17.6 %all-to-all-done.1.refs_4_.refs_2_ = f32[32,2,32,128]{3,2,1,0:T(8,128)S(1)} async-done(((f32[32,2,32,128]{3,2,1,0:T(8,128)}), f32[32,2,32,128]{3,2,1,0:T(8,128)S(1)}, u32[]{:S(2)}, u32[]{:S(2)}) %all-to-all-start.1) | async-done | bytes 1048608 | tf_op jit(solution)/shard_map/all_to_all | solution.py:162
  69.2 3.6 %shard_map.88 = (bf16[128,1024]{1,0:T(8,128)(2,1)}, f32[8,128,128]{2,1,0:T(8,128)}) custom-call(bf16[128,1024]{1,0:T(8,128)(2,1)} %bitcast.21, f32[128,1024]{1,0:T(8,128)} %get-tuple-element.19.refs_1_, f32[32,2,32,128]{3,2,1,0:T(8,128)} %copy-done, bf16[1024,1024]{1,0:T(8,128)(2,1)} %fusion.refs_3_), custom_call_target="tpu_custom_call" | custom-call | tf_op jit(solution)/shard_map/pallas_call | solution.py:28
  72.8 17.1 %all-to-all-start.2 = ((f32[8,128,128]{2,1,0:T(8,128)}), f32[8,128,128]{2,1,0:T(8,128)S(1)}, u32[]{:S(2)}, u32[]{:S(2)}) async-start(f32[8,128,128]{2,1,0:T(8,128)} %get-tuple-element.25), calls=%async_computation.2 | async-start | bytes 1048576 | tf_op jit(solution)/shard_map/all_to_all | solution.py:162
  89.9 5.1 %collective-permute-start.5 = (f32[128,1152]{1,0:T(8,128)S(1)}, f32[128,1152]{1,0:T(8,128)S(1)}, u32[]{:S(2)}, u32[]{:S(2)}) collective-permute-start(f32[128,1152]{1,0:T(8,128)S(1)} %bitcast_convert_fusion.refs_0_), channel_id=1, source_target_pairs={{0,192},{64,0},{128,64},{192,128},{1,193},{65,1},{129,65},{193,129... | collective-permute-start | bytes 1769480 | tf_op jit(solution)/shard_map/ppermute | solution.py:170
  95.0 1.9 collective-permute-start.3
  96.9 2.5 %collective-permute-start.1 = (f32[128,1152]{1,0:T(8,128)S(1)}, f32[128,1152]{1,0:T(8,128)S(1)}, u32[]{:S(2)}, u32[]{:S(2)}) collective-permute-start(f32[128,1152]{1,0:T(8,128)S(1)} %bitcast_convert_fusion.refs_0_), channel_id=1, source_target_pairs={{0,64},{64,128},{128,192},{192,0},{1,65},{65,129},{129,193},{193,1... | collective-permute-start | bytes 1769480 | tf_op jit(solution)/shard_map/ppermute | solution.py:170
  99.4 3.1 %collective-permute-start = (f32[128,1152]{1,0:T(8,128)S(1)}, f32[128,1152]{1,0:T(8,128)S(1)}, u32[]{:S(2)}, u32[]{:S(2)}) collective-permute-start(f32[128,1152]{1,0:T(8,128)S(1)} %bitcast_convert_fusion.refs_0_), channel_id=1, source_target_pairs={{0,32},{32,0},{1,33},{33,1},{2,34},{34,2},{3,35},{35,3},{4,36},{36... | collective-permute-start | bytes 1769480 | tf_op jit(solution)/shard_map/ppermute | solution.py:168
  102.6 10.6 %collective-permute-done.5.refs_6_ = f32[128,1152]{1,0:T(8,128)S(1)} collective-permute-done((f32[128,1152]{1,0:T(8,128)S(1)}, f32[128,1152]{1,0:T(8,128)S(1)}, u32[]{:S(2)}, u32[]{:S(2)}) %collective-permute-start.5) | collective-permute-done | bytes 589856 | tf_op jit(solution)/shard_map/ppermute | solution.py:170
  113.2 2.9 %collective-permute-start.6 = (f32[128,1152]{1,0:T(8,128)S(1)}, f32[128,1152]{1,0:T(8,128)}, u32[]{:S(2)}, u32[]{:S(2)}) collective-permute-start(f32[128,1152]{1,0:T(8,128)S(1)} %collective-permute-done.5.refs_6_), channel_id=1, source_target_pairs={{0,32},{32,0},{1,33},{33,1},{2,34},{34,2},{3,35},{35,3},{4,36},{36... | collective-permute-start | bytes 1769480 | tf_op jit(solution)/shard_map/ppermute | solution.py:171
  116.1 38.8 %collective-permute-done.3.refs_4_ = f32[128,1152]{1,0:T(8,128)S(1)} collective-permute-done((f32[128,1152]{1,0:T(8,128)S(1)}, f32[128,1152]{1,0:T(8,128)S(1)}, u32[]{:S(2)}, u32[]{:S(2)}) %collective-permute-start.3) | collective-permute-done | bytes 589856 | tf_op jit(solution)/shard_map/ppermute | solution.py:170
  154.9 2.9 %collective-permute-start.4 = (f32[128,1152]{1,0:T(8,128)S(1)}, f32[128,1152]{1,0:T(8,128)}, u32[]{:S(2)}, u32[]{:S(2)}) collective-permute-start(f32[128,1152]{1,0:T(8,128)S(1)} %collective-permute-done.3.refs_4_), channel_id=1, source_target_pairs={{0,32},{32,0},{1,33},{33,1},{2,34},{34,2},{3,35},{35,3},{4,36},{36... | collective-permute-start | bytes 1769480 | tf_op jit(solution)/shard_map/ppermute | solution.py:171
  157.8 1.9 collective-permute-start.2
  161.8 4.0 %shard_map.89.refs_2_ = bf16[8,128,1152]{2,1,0:T(8,128)(2,1)} custom-call(f32[128,1152]{1,0:T(8,128)} %copy-done.1, f32[128,1152]{1,0:T(8,128)} %copy-done.6, f32[128,1152]{1,0:T(8,128)} %copy-done.5, f32[128,1152]{1,0:T(8,128)} %collective-permute-done.2.refs_3_, f32[128,1152]{1,0:T(8,128)} %copy-done.4, f32[128,1152]{1,0:T(8,128)} %collective-permute-done.4.refs_5_, ...), custom_call_target="tpu_custom_call" | custom-call | tf_op jit(solution)/shard_map/pallas_call | solution.py:28
  166.6 3.5 %weight.1 = f32[32,4,1152]{2,1,0:T(4,128)} custom-call(s32[2]{0:T(128)} %pad_add_fusion.refs_0_, f32[8,128,128]{2,1,0:T(8,128)} %copy-done.2, bf16[8,128,1152]{2,1,0:T(8,128)(2,1)} %shard_map.89.refs_2_), custom_call_target="tpu_custom_call" | custom-call | tf_op jit(solution)/shard_map/weight/pallas_call | solution.py:189
  170.1 23.1 %all_to_all.26.in_ref = f32[32,4,1152]{2,1,0:T(4,128)} all-to-all(f32[32,4,1152]{2,1,0:T(4,128)} %weight.1), channel_id=1, replica_groups=mesh['a'=3,'b'=4,'c'=2,'x'=4,'y'=8] {'x','y'}, dimensions={0} | all-to-all | bytes 1179648 | tf_op jit(solution)/shard_map/all_to_all | solution.py:162
  193.2 1.9 shard_map.90
  195.0 13.1 %all-to-all-start.4 = ((f32[24,1,192]{2,1,0:T(1,128)}), f32[24,1,192]{2,1,0:T(1,128)S(1)}, u32[]{:S(2)}, u32[]{:S(2)}) async-start(f32[24,1,192]{2,1,0:T(1,128)} %shard_map.90), calls=%async_computation.4 | async-start | bytes 49152 | tf_op jit(solution)/shard_map/all_to_all | solution.py:162
  208.2 3.0 %shard_map.87 = (bf16[128,1024]{1,0:T(8,128)(2,1)}, bf16[128,1024]{1,0:T(8,128)(2,1)}) custom-call(bf16[128,1024]{1,0:T(8,128)(2,1)} %bitcast.15, bf16[128,1024]{1,0:T(8,128)(2,1)} %bitcast.18, f32[128,1024]{1,0:T(8,128)} %get-tuple-element.15.refs_2_, f32[128,1024]{1,0:T(8,128)} %get-tuple-element.16.refs_3_, f32[32,2,32,128]{3,2,1,0:T(8,128)} %copy-done), custom_call_target="tpu_custom_call" | custom-call | tf_op jit(solution)/shard_map/pallas_call | solution.py:28
  211.2 6.8 %all-to-all-done.4.refs_0_ = f32[24,1,192]{2,1,0:T(1,128)S(1)} async-done(((f32[24,1,192]{2,1,0:T(1,128)}), f32[24,1,192]{2,1,0:T(1,128)S(1)}, u32[]{:S(2)}, u32[]{:S(2)}) %all-to-all-start.4) | async-done | bytes 18464 | tf_op jit(solution)/shard_map/all_to_all | solution.py:162
  (29 shorter events, 7.7 us)
Async XLA Ops:
  39.3 28.9 %all-to-all-start.1 = ((f32[32,2,32,128]{3,2,1,0:T(8,128)}), f32[32,2,32,128]{3,2,1,0:T(8,128)S(1)}, u32[]{:S(2)}, u32[]{:S(2)}) async-start(f32[32,2,32,128]{3,2,1,0:T(8,128)} %shard_map.86), calls=%async_computation.1 | async-start | bytes 2097152 | tf_op jit(solution)/shard_map/all_to_all | solution.py:162
  68.2 1.0 copy-start
  69.2 20.7 %copy-start.7 = (bf16[1,128,1152]{2,1,0:T(8,128)(2,1)S(1)}, bf16[1,128,1152]{2,1,0:T(8,128)(2,1)}, u32[]{:S(2)}) copy-start(bf16[1,128,1152]{2,1,0:T(8,128)(2,1)} %param.13) | copy-start | bytes 884740
  72.8 93.0 %all-to-all-start.2 = ((f32[8,128,128]{2,1,0:T(8,128)}), f32[8,128,128]{2,1,0:T(8,128)S(1)}, u32[]{:S(2)}, u32[]{:S(2)}) async-start(f32[8,128,128]{2,1,0:T(8,128)} %get-tuple-element.25), calls=%async_computation.2 | async-start | bytes 1048576 | tf_op jit(solution)/shard_map/all_to_all | solution.py:162
  89.9 71.8 %copy-start.1 = (f32[128,1152]{1,0:T(8,128)}, f32[128,1152]{1,0:T(8,128)S(1)}, u32[]{:S(2)}) copy-start(f32[128,1152]{1,0:T(8,128)S(1)} %bitcast_convert_fusion.refs_0_) | copy-start | bytes 1769476
  89.9 23.2 %collective-permute-start.5 = (f32[128,1152]{1,0:T(8,128)S(1)}, f32[128,1152]{1,0:T(8,128)S(1)}, u32[]{:S(2)}, u32[]{:S(2)}) collective-permute-start(f32[128,1152]{1,0:T(8,128)S(1)} %bitcast_convert_fusion.refs_0_), channel_id=1, source_target_pairs={{0,192},{64,0},{128,64},{192,128},{1,193},{65,1},{129,65},{193,129... | collective-permute-start | bytes 1769480 | tf_op jit(solution)/shard_map/ppermute | solution.py:170
  95.0 59.8 %collective-permute-start.3 = (f32[128,1152]{1,0:T(8,128)S(1)}, f32[128,1152]{1,0:T(8,128)S(1)}, u32[]{:S(2)}, u32[]{:S(2)}) collective-permute-start(f32[128,1152]{1,0:T(8,128)S(1)} %bitcast_convert_fusion.refs_0_), channel_id=1, source_target_pairs={{0,128},{64,192},{128,0},{192,64},{1,129},{65,193},{129,1},{193,65... | collective-permute-start | bytes 1769480 | tf_op jit(solution)/shard_map/ppermute | solution.py:170
  96.9 60.8 %collective-permute-start.1 = (f32[128,1152]{1,0:T(8,128)S(1)}, f32[128,1152]{1,0:T(8,128)S(1)}, u32[]{:S(2)}, u32[]{:S(2)}) collective-permute-start(f32[128,1152]{1,0:T(8,128)S(1)} %bitcast_convert_fusion.refs_0_), channel_id=1, source_target_pairs={{0,64},{64,128},{128,192},{192,0},{1,65},{65,129},{129,193},{193,1... | collective-permute-start | bytes 1769480 | tf_op jit(solution)/shard_map/ppermute | solution.py:170
  99.4 60.9 %collective-permute-start = (f32[128,1152]{1,0:T(8,128)S(1)}, f32[128,1152]{1,0:T(8,128)S(1)}, u32[]{:S(2)}, u32[]{:S(2)}) collective-permute-start(f32[128,1152]{1,0:T(8,128)S(1)} %bitcast_convert_fusion.refs_0_), channel_id=1, source_target_pairs={{0,32},{32,0},{1,33},{33,1},{2,34},{34,2},{3,35},{35,3},{4,36},{36... | collective-permute-start | bytes 1769480 | tf_op jit(solution)/shard_map/ppermute | solution.py:168
  113.2 48.6 %copy-start.3 = (f32[128,1152]{1,0:T(8,128)}, f32[128,1152]{1,0:T(8,128)S(1)}, u32[]{:S(2)}) copy-start(f32[128,1152]{1,0:T(8,128)S(1)} %collective-permute-done.5.refs_6_) | copy-start | bytes 1769476
  113.2 47.1 %collective-permute-start.6 = (f32[128,1152]{1,0:T(8,128)S(1)}, f32[128,1152]{1,0:T(8,128)}, u32[]{:S(2)}, u32[]{:S(2)}) collective-permute-start(f32[128,1152]{1,0:T(8,128)S(1)} %collective-permute-done.5.refs_6_), channel_id=1, source_target_pairs={{0,32},{32,0},{1,33},{33,1},{2,34},{34,2},{3,35},{35,3},{4,36},{36... | collective-permute-start | bytes 1769480 | tf_op jit(solution)/shard_map/ppermute | solution.py:171
  154.9 6.9 %copy-start.4 = (f32[128,1152]{1,0:T(8,128)}, f32[128,1152]{1,0:T(8,128)S(1)}, u32[]{:S(2)}) copy-start(f32[128,1152]{1,0:T(8,128)S(1)} %collective-permute-done.3.refs_4_) | copy-start | bytes 1769476
  154.9 5.4 %collective-permute-start.4 = (f32[128,1152]{1,0:T(8,128)S(1)}, f32[128,1152]{1,0:T(8,128)}, u32[]{:S(2)}, u32[]{:S(2)}) collective-permute-start(f32[128,1152]{1,0:T(8,128)S(1)} %collective-permute-done.3.refs_4_), channel_id=1, source_target_pairs={{0,32},{32,0},{1,33},{33,1},{2,34},{34,2},{3,35},{35,3},{4,36},{36... | collective-permute-start | bytes 1769480 | tf_op jit(solution)/shard_map/ppermute | solution.py:171
  157.7 4.1 %copy-start.5 = (f32[128,1152]{1,0:T(8,128)}, f32[128,1152]{1,0:T(8,128)S(1)}, u32[]{:S(2)}) copy-start(f32[128,1152]{1,0:T(8,128)S(1)} %collective-permute-done.1.refs_2_) | copy-start | bytes 1769476
  157.8 4.0 %collective-permute-start.2 = (f32[128,1152]{1,0:T(8,128)S(1)}, f32[128,1152]{1,0:T(8,128)}, u32[]{:S(2)}, u32[]{:S(2)}) collective-permute-start(f32[128,1152]{1,0:T(8,128)S(1)} %collective-permute-done.1.refs_2_), channel_id=1, source_target_pairs={{0,32},{32,0},{1,33},{33,1},{2,34},{34,2},{3,35},{35,3},{4,36},{36... | collective-permute-start | bytes 1769480 | tf_op jit(solution)/shard_map/ppermute | solution.py:171
  160.3 1.5 copy-start.6
  165.8 0.8 copy-start.2
  195.0 22.9 %all-to-all-start.4 = ((f32[24,1,192]{2,1,0:T(1,128)}), f32[24,1,192]{2,1,0:T(1,128)S(1)}, u32[]{:S(2)}, u32[]{:S(2)}) async-start(f32[24,1,192]{2,1,0:T(1,128)} %shard_map.90), calls=%async_computation.4 | async-start | bytes 49152 | tf_op jit(solution)/shard_map/all_to_all | solution.py:162
  218.0 0.6 copy-start.8
where the time goes:
time: 221 us; the launch traced here: 220 us
  waiting for transfers between devices  75.3 us (34%)
  blocking collectives  57 us (26%)
  starting transfers between devices  55.8 us (25%)
  Pallas kernels  26.4 us (12%)
  local copies, waits for them, and re-layouts  2.42 us (1%)
  other arithmetic  2.38 us (1%)
    all_to_all x2, blocking collectives, exchange(): return lax.all_to_all(array, axes, 0, 0, tiled=True)  57 us
    ppermute x3, waiting for transfers between devices, on_device(): array = lax.ppermute(own, 'b', [(i, (i + d) % nb) for i in range(nb)])  49.4 us
    all_to_all x3, starting transfers between devices, exchange(): return lax.all_to_all(array, axes, 0, 0, tiled=True)  35.5 us
    all_to_all x3, waiting for transfers between devices, exchange(): return lax.all_to_all(array, axes, 0, 0, tiled=True)  24.4 us
    pallas_call x8, Pallas kernels, call(): return pl.pallas_call(body, out_shape=outs, interpret=INTERPRET)(*args)  22.9 us
    ppermute x3, starting transfers between devices, on_device(): array = lax.ppermute(own, 'b', [(i, (i + d) % nb) for i in range(nb)])  9.44 us
    ppermute x3, starting transfers between devices, on_device(): both += [array, lax.ppermute(array, 'c', swap)]  7.66 us
  transfers between devices with their start and end apart: 10, of which 5 were waited for; matrix products, arithmetic and copies ran while one was open for 1% of the time, Pallas kernels for 5%

commit v1 on v0

v1 whole, which is shorter than its diff:
```python
import math

import jax
import jax.numpy as jnp
from jax import lax
from jax.experimental import pallas as pl
from jax.experimental.pallas import tpu as pltpu
from jax.sharding import Mesh
from jax.sharding import PartitionSpec as P

HD = 128
HV = 8
DW = 1152
TOK = 128
VW = HV * HD
BF = jnp.bfloat16
F32 = jnp.float32
INTERPRET = False


def dot(a, b, ca, cb):
    if INTERPRET:
        a, b = a.astype(F32), b.astype(F32)
    return lax.dot_general(a, b, (((ca,), (cb,)), ((), ())), preferred_element_type=F32)


def call(body, outs, *args):
    return pl.pallas_call(body, out_shape=outs, interpret=INTERPRET)(*args)


def head(h):
    return slice(h * HD, (h + 1) * HD)


def states_body(q_ref, k_ref, v_ref, g_ref, st_ref):
    rows = st_ref.shape[1] // 2
    for h in range(HV):
        s = head(h)
        for which, (a_ref, b_ref) in enumerate(((k_ref, v_ref), (q_ref, g_ref))):
            block = dot(a_ref[:, s], b_ref[:, s], 0, 0)
            at = which * rows
            if rows <= HD:
                per = HD // rows
                st_ref[h * per : (h + 1) * per, at : at + rows] = block.reshape(per, rows, HD)
            else:
                at += h * HD % rows
                st_ref[h * HD // rows, at : at + HD] = block


def load_state(st_ref, which, h):
    rows = st_ref.shape[1] // 2
    at = which * rows
    if rows <= HD:
        per = HD // rows
        block = st_ref[h * per : (h + 1) * per, at : at + rows].reshape(HD, HD)
    else:
        at += h * HD % rows
        block = st_ref[h * HD // rows, at : at + HD]
    return block.astype(BF)


def intra_body(scale, q_ref, k_ref, v_ref, g_ref, dq_ref, dk_ref, dv_ref):
    t = lax.broadcasted_iota(jnp.int32, (TOK, TOK), 0)
    u = lax.broadcasted_iota(jnp.int32, (TOK, TOK), 1)
    causal = t >= u
    for h in range(HV):
        s = head(h)
        q, k, v, g = q_ref[:, s], k_ref[:, s], v_ref[:, s], g_ref[:, s]
        score_w = jnp.where(causal, scale * dot(q, k, 1, 1), 0.0).astype(BF)
        grad_w = jnp.where(causal, scale * dot(g, v, 1, 1), 0.0).astype(BF)
        dq_ref[:, s] = dot(grad_w, k, 1, 0)
        dk_ref[:, s] = dot(grad_w, q, 0, 0)
        dv_ref[:, s] = dot(score_w, g, 0, 0)


def scan_body(in_ref, out_ref):
    n, rows = in_ref.shape[0], in_ref.shape[1] // 2
    for which, order in enumerate((range(n), range(n)[::-1])):
        part = slice(which * rows, (which + 1) * rows)
        total = jnp.zeros((rows, HD), F32)
        for i in order:
            out_ref[i, part] = total
            total = total + in_ref[i, part]


def value_body(scale, k_ref, dvi_ref, st_ref, perm_ref, dv_ref, send_ref):
    for h in range(HV):
        s = head(h)
        inter = dot(k_ref[:, s], load_state(st_ref, 1, h), 1, 0)
        dv_ref[:, s] = (dvi_ref[:, s] + scale * inter).astype(BF)
    wide = perm_ref.shape[0]
    for b in range(VW // wide):
        moved = dot(dv_ref[:, b * wide : (b + 1) * wide], perm_ref[...], 1, 0)
        send_ref[2 * b] = moved[:, : wide // 2]
        send_ref[2 * b + 1] = moved[:, wide // 2 :]


def outer_body(scale, g_ref, v_ref, dqi_ref, dki_ref, st_ref, dq_ref, dk_ref):
    for h in range(HV):
        s = head(h)
        inter = dot(g_ref[:, s], load_state(st_ref, 0, h), 1, 1)
        dq_ref[:, s] = (dqi_ref[:, s] + scale * inter).astype(BF)
        inter = dot(v_ref[:, s], load_state(st_ref, 1, h), 1, 1)
        dk_ref[:, s] = (dki_ref[:, s] + scale * inter).astype(BF)


def pack_body(*refs):
    for i, ref in enumerate(refs[:-1]):
        refs[-1][i] = ref[...].astype(BF)


def weight_body(rscale, place_ref, dv_ref, x_ref, out_ref):
    n = dv_ref.shape[0] // 2
    columns = []
    for i in range(2 * n):
        slot = 2 * lax.rem(place_ref[0] + n - i // 2, n) + lax.rem(place_ref[1] + i % 2, 2)
        columns.append(dv_ref[slot].astype(BF))
    tokens = x_ref[...].reshape(2 * n * TOK, DW)
    out_ref[...] = dot(jnp.concatenate(columns, axis=0), tokens, 0, 0) * rscale


def fold_body(in_ref, out_ref):
    total = in_ref[0]
    for i in range(1, in_ref.shape[0]):
        total = total + in_ref[i]
    n, half, wide = out_ref.shape
    rows = wide // 2
    for i in range(n):
        part = total[:, i * rows : (i + 1) * rows]
        out_ref[i] = jnp.concatenate([part[:half], part[half:]], axis=1)


def last_body(in_ref, out_ref):
    n, half, wide = in_ref.shape
    rows = wide // 2
    for c in range(2):
        total = in_ref[c]
        for z in range(1, n // 2):
            total = total + in_ref[2 * z + c]
        at = 2 * c * half
        out_ref[at : at + half] = total[:, :rows]
        out_ref[at + half : at + 2 * half] = total[:, rows:]


def on_device(sizes, query_heads, key_heads, value_heads, grad_output, layer_input):
    nz, nx, ny = sizes
    nc = nx * ny
    length = TOK * nc
    scale = 1.0 / math.sqrt(HD * length)
    rscale = 1.0 / math.sqrt(2 * nz * length)
    q, k, v, g = query_heads[0], key_heads[0], value_heads[0], grad_output[0]
    wide = VW // nx
    width = wide // ny
    half = width // 2

    def shaped(*shape, dtype=F32):
        return jax.ShapeDtypeStruct(shape, dtype)

    states = shaped(nc, 2 * VW // nc, HD)
    flat = shaped(TOK, VW)
    flat_bf = shaped(TOK, VW, dtype=BF)

    def exchange(array, axes):
        return lax.all_to_all(array, axes, 0, 0, tiled=True)

    held = exchange(call(states_body, states, q, k, v, g), ("x", "y"))

    own = layer_input[0].astype(F32)
    swap = [(0, 1), (1, 0)]
    both = [own, lax.ppermute(own, "c", swap)]
    for d in range(1, nx):
        array = lax.ppermute(own, "x", [(i, (i + d) % nx) for i in range(nx)])
        both += [array, lax.ppermute(array, "c", swap)]
    inputs = call(pack_body, shaped(2 * nx, TOK, DW, dtype=BF), *both)
    place = jnp.stack([lax.axis_index("x"), lax.axis_index("c")]).astype(jnp.int32)

    dqi, dki, dvi = call(lambda *refs: intra_body(scale, *refs), [flat] * 3, q, k, v, g)
    at = jnp.arange(wide)
    to = at % width // half * (wide // 2) + at // width * half + at % half
    perm = (at[None, :] == to[:, None]).astype(BF)

    state = exchange(call(scan_body, states, held), ("x", "y"))
    dv, send = call(
        lambda *refs: value_body(scale, *refs),
        [flat_bf, shaped(2 * nx, TOK, wide // 2)],
        k, dvi, state, perm,
    )
    columns = exchange(send, ("x", "c"))
    dq, dk = call(lambda *refs: outer_body(scale, *refs), [flat_bf] * 2, g, v, dqi, dki, state)
    term = pl.pallas_call(
        lambda *refs: weight_body(rscale, *refs),
        in_specs=[pl.BlockSpec(memory_space=pltpu.SMEM)] + [pl.BlockSpec(memory_space=pltpu.VMEM)] * 2,
        out_shape=shaped(wide // 2, DW),
        name="weight",
        interpret=INTERPRET,
    )(place, columns, inputs)
    terms = exchange(term.reshape(ny, half, DW), "y")
    rows = DW // (2 * nz)
    folded = call(fold_body, shaped(2 * nz, half // 2, 2 * rows), terms)
    parts = exchange(folded, ("z", "c"))
    weight = call(last_body, shaped(width, rows), parts)
    return dq[None], dk[None], dv[None], weight.T


def solution(mesh):
    nx = SHAPE_X
    sizes = (mesh.shape["dp"] // 2, nx, mesh.shape["ctx"] // nx)
    inner = Mesh(mesh.devices.reshape(sizes[0], 2, *sizes[1:]), ("z", "c", "x", "y"))
    spec = P(("z", "c"), ("x", "y"), None)

    def body(*arrays):
        return on_device(sizes, *arrays)

    return jax.shard_map(
        body,
        mesh=inner,
        in_specs=(spec,) * 5,
        out_specs=(spec, spec, spec, P(("z", "c"), ("x", "y"))),
        check_vma=False,
    )


SHAPE_X = 4
```

time: 221 us -> 174 us (0.79)
  the two profiles are of different devices: /device:TPU:9 before, /device:TPU:1 now
where the time goes in v1:
time: 174 us; the launch traced here: 172 us
  starting transfers between devices  70 us (40%)
  blocking collectives  53.8 us (31%)
  Pallas kernels  25.3 us (15%)
  waiting for transfers between devices  18.7 us (11%)
  local copies, waits for them, and re-layouts  2.43 us (1%)
    all_to_all x2, blocking collectives, exchange(): return lax.all_to_all(array, axes, 0, 0, tiled=True)  53.8 us
    all_to_all x3, starting transfers between devices, exchange(): return lax.all_to_all(array, axes, 0, 0, tiled=True)  33.9 us
    pallas_call x8, Pallas kernels, call(): return pl.pallas_call(body, out_shape=outs, interpret=INTERPRET)(*args)  22.1 us
    ppermute x3, starting transfers between devices, on_device(): both += [array, lax.ppermute(array, 'c', swap)]  17.4 us
    all_to_all x3, waiting for transfers between devices, exchange(): return lax.all_to_all(array, axes, 0, 0, tiled=True)  12.8 us
    ppermute x3, starting transfers between devices, on_device(): array = lax.ppermute(own, 'x', [(i, (i + d) % nx) for i in range(nx)])  10.5 us
    ppermute x1, starting transfers between devices, on_device(): both = [own, lax.ppermute(own, 'c', swap)]  8.2 us
    ppermute x3, waiting for transfers between devices, on_device(): array = lax.ppermute(own, 'x', [(i, (i + d) % nx) for i in range(nx)])  5.93 us
  transfers between devices with their start and end apart: 10, of which 4 were waited for; matrix products, arithmetic and copies ran while one was open for 1% of the time, Pallas kernels for 8%

profile of v1, /device:TPU:1, one launch (start us, length us, event | category | flops | bytes accessed | tf_op | source)
XLA Modules:
  0.0 172.5 jit_solution(12974508173145805185)
XLA Ops:
  0.6 2.5 %shard_map.85 = f32[32,64,128]{2,1,0:T(8,128)} custom-call(bf16[128,1024]{1,0:T(8,128)(2,1)} %bitcast.24, bf16[128,1024]{1,0:T(8,128)(2,1)} %bitcast.15, bf16[128,1024]{1,0:T(8,128)(2,1)} %bitcast.21, bf16[128,1024]{1,0:T(8,128)(2,1)} %bitcast.18), custom_call_target="tpu_custom_call" | custom-call | tf_op jit(solution)/shard_map/pallas_call | solution.py:28
  3.1 30.9 %all_to_all.25.in_ref = f32[32,64,128]{2,1,0:T(8,128)} all-to-all(f32[32,64,128]{2,1,0:T(8,128)} %shard_map.85), channel_id=1, replica_groups=mesh['z'=12,'c'=2,'x'=4,'y'=8] {'x','y'}, dimensions={0} | all-to-all | bytes 2097152 | tf_op jit(solution)/shard_map/all_to_all | solution.py:164
  34.0 2.3 %shard_map.86 = f32[32,64,128]{2,1,0:T(8,128)} custom-call(f32[32,64,128]{2,1,0:T(8,128)} %all_to_all.25.in_ref), custom_call_target="tpu_custom_call" | custom-call | tf_op jit(solution)/shard_map/pallas_call | solution.py:28
  36.4 9.2 %all-to-all-start.1 = ((f32[32,64,128]{2,1,0:T(8,128)}), f32[32,64,128]{2,1,0:T(8,128)S(1)}, u32[]{:S(2)}, u32[]{:S(2)}) async-start(f32[32,64,128]{2,1,0:T(8,128)} %shard_map.86), calls=%async_computation.1 | async-start | bytes 2097152 | tf_op jit(solution)/shard_map/all_to_all | solution.py:164
  45.6 3.1 %collective-permute-start.1 = (f32[128,1152]{1,0:T(8,128)S(1)}, f32[128,1152]{1,0:T(8,128)S(1)}, u32[]{:S(2)}, u32[]{:S(2)}) collective-permute-start(f32[128,1152]{1,0:T(8,128)S(1)} %bitcast_convert_fusion.refs_0_), channel_id=1, source_target_pairs={{0,8},{8,16},{16,24},{24,0},{1,9},{9,17},{17,25},{25,1},{2,10},{10... | collective-permute-start | bytes 1769480 | tf_op jit(solution)/shard_map/ppermute | solution.py:172
  48.8 4.3 %collective-permute-start.3 = (f32[128,1152]{1,0:T(8,128)S(1)}, f32[128,1152]{1,0:T(8,128)S(1)}, u32[]{:S(2)}, u32[]{:S(2)}) collective-permute-start(f32[128,1152]{1,0:T(8,128)S(1)} %bitcast_convert_fusion.refs_0_), channel_id=1, source_target_pairs={{0,16},{8,24},{16,0},{24,8},{1,17},{9,25},{17,1},{25,9},{2,18},{10... | collective-permute-start | bytes 1769480 | tf_op jit(solution)/shard_map/ppermute | solution.py:172
  53.1 3.1 %collective-permute-start.5 = (f32[128,1152]{1,0:T(8,128)S(1)}, f32[128,1152]{1,0:T(8,128)S(1)}, u32[]{:S(2)}, u32[]{:S(2)}) collective-permute-start(f32[128,1152]{1,0:T(8,128)S(1)} %bitcast_convert_fusion.refs_0_), channel_id=1, source_target_pairs={{0,24},{8,0},{16,8},{24,16},{1,25},{9,1},{17,9},{25,17},{2,26},{10... | collective-permute-start | bytes 1769480 | tf_op jit(solution)/shard_map/ppermute | solution.py:172
  56.2 8.2 %collective-permute-start = (f32[128,1152]{1,0:T(8,128)S(1)}, f32[128,1152]{1,0:T(8,128)}, u32[]{:S(2)}, u32[]{:S(2)}) collective-permute-start(f32[128,1152]{1,0:T(8,128)S(1)} %bitcast_convert_fusion.refs_0_), channel_id=1, source_target_pairs={{0,32},{32,0},{1,33},{33,1},{2,34},{34,2},{3,35},{35,3},{4,36},{36... | collective-permute-start | bytes 1769480 | tf_op jit(solution)/shard_map/ppermute | solution.py:170
  64.4 4.2 %shard_map.84 = (f32[128,1024]{1,0:T(8,128)}, f32[128,1024]{1,0:T(8,128)}, f32[128,1024]{1,0:T(8,128)}) custom-call(bf16[128,1024]{1,0:T(8,128)(2,1)} %bitcast.25, bf16[128,1024]{1,0:T(8,128)(2,1)} %bitcast.16, bf16[128,1024]{1,0:T(8,128)(2,1)} %bitcast.22, bf16[128,1024]{1,0:T(8,128)(2,1)} %bitcast.19), custom_call_target="tpu_custom_call" | custom-call | tf_op jit(solution)/shard_map/pallas_call | solution.py:28
  69.9 9.8 %collective-permute-start.2 = (f32[128,1152]{1,0:T(8,128)S(1)}, f32[128,1152]{1,0:T(8,128)}, u32[]{:S(2)}, u32[]{:S(2)}) collective-permute-start(f32[128,1152]{1,0:T(8,128)S(1)} %collective-permute-done.1.refs_2_), channel_id=1, source_target_pairs={{0,32},{32,0},{1,33},{33,1},{2,34},{34,2},{3,35},{35,3},{4,36},{36... | collective-permute-start | bytes 1769480 | tf_op jit(solution)/shard_map/ppermute | solution.py:173
  79.7 4.7 %collective-permute-done.3.refs_4_ = f32[128,1152]{1,0:T(8,128)S(1)} collective-permute-done((f32[128,1152]{1,0:T(8,128)S(1)}, f32[128,1152]{1,0:T(8,128)S(1)}, u32[]{:S(2)}, u32[]{:S(2)}) %collective-permute-start.3) | collective-permute-done | bytes 589856 | tf_op jit(solution)/shard_map/ppermute | solution.py:172
  84.5 5.6 %collective-permute-start.4 = (f32[128,1152]{1,0:T(8,128)S(1)}, f32[128,1152]{1,0:T(8,128)}, u32[]{:S(2)}, u32[]{:S(2)}) collective-permute-start(f32[128,1152]{1,0:T(8,128)S(1)} %collective-permute-done.3.refs_4_), channel_id=1, source_target_pairs={{0,32},{32,0},{1,33},{33,1},{2,34},{34,2},{3,35},{35,3},{4,36},{36... | collective-permute-start | bytes 1769480 | tf_op jit(solution)/shard_map/ppermute | solution.py:173
  90.1 1.9 %collective-permute-start.6 = (f32[128,1152]{1,0:T(8,128)S(1)}, f32[128,1152]{1,0:T(8,128)}, u32[]{:S(2)}, u32[]{:S(2)}) collective-permute-start(f32[128,1152]{1,0:T(8,128)S(1)} %collective-permute-done.5.refs_6_), channel_id=1, source_target_pairs={{0,32},{32,0},{1,33},{33,1},{2,34},{34,2},{3,35},{35,3},{4,36},{36... | collective-permute-start | bytes 1769480 | tf_op jit(solution)/shard_map/ppermute | solution.py:173
  93.8 2.6 %shard_map.88 = (bf16[128,1024]{1,0:T(8,128)(2,1)}, f32[8,128,128]{2,1,0:T(8,128)}) custom-call(bf16[128,1024]{1,0:T(8,128)(2,1)} %bitcast.17, f32[128,1024]{1,0:T(8,128)} %get-tuple-element.15.refs_1_, f32[32,64,128]{2,1,0:T(8,128)} %copy-done, bf16[256,256]{1,0:T(8,128)(2,1)} %fusion.refs_3_), custom_call_target="tpu_custom_call" | custom-call | tf_op jit(solution)/shard_map/pallas_call | solution.py:28
  96.4 3.9 %all-to-all-start.2 = ((f32[8,128,128]{2,1,0:T(8,128)}), f32[8,128,128]{2,1,0:T(8,128)S(1)}, u32[]{:S(2)}, u32[]{:S(2)}) async-start(f32[8,128,128]{2,1,0:T(8,128)} %get-tuple-element.17), calls=%async_computation.2 | async-start | bytes 1048576 | tf_op jit(solution)/shard_map/all_to_all | solution.py:164
  100.9 4.0 %shard_map.89.refs_2_ = bf16[8,128,1152]{2,1,0:T(8,128)(2,1)} custom-call(f32[128,1152]{1,0:T(8,128)} %copy-done.1, f32[128,1152]{1,0:T(8,128)} %collective-permute-done.refs_1_, f32[128,1152]{1,0:T(8,128)} %copy-done.3, f32[128,1152]{1,0:T(8,128)} %collective-permute-done.2.refs_3_, f32[128,1152]{1,0:T(8,128)} %copy-done.4, ...), custom_call_target="tpu_custom_call" | custom-call | tf_op jit(solution)/shard_map/pallas_call | solution.py:28
  104.9 4.7 %all-to-all-done.2.refs_1_ = f32[8,128,128]{2,1,0:T(8,128)S(1)} async-done(((f32[8,128,128]{2,1,0:T(8,128)}), f32[8,128,128]{2,1,0:T(8,128)S(1)}, u32[]{:S(2)}, u32[]{:S(2)}) %all-to-all-start.2) | async-done | bytes 524320 | tf_op jit(solution)/shard_map/all_to_all | solution.py:164
  110.5 3.2 %weight.1 = f32[128,1152]{1,0:T(8,128)} custom-call(s32[2]{0:T(128)} %pad_add_fusion.refs_0_, f32[8,128,128]{2,1,0:T(8,128)} %copy-done.2, bf16[8,128,1152]{2,1,0:T(8,128)(2,1)} %shard_map.89.refs_2_), custom_call_target="tpu_custom_call" | custom-call | tf_op jit(solution)/shard_map/weight/pallas_call | solution.py:190
  113.7 22.9 %all_to_all.26.in_ref = f32[8,16,1152]{2,1,0:T(8,128)} all-to-all(f32[8,16,1152]{2,1,0:T(8,128)} %bitcast.14), channel_id=1, replica_groups=mesh['z'=12,'c'=2,'x'=4,'y'=8] {'y'}, dimensions={0} | all-to-all | bytes 1179648 | tf_op jit(solution)/shard_map/all_to_all | solution.py:164
  136.6 1.8 %shard_map.90 = f32[24,8,96]{2,1,0:T(8,128)} custom-call(f32[8,16,1152]{2,1,0:T(8,128)} %all_to_all.26.in_ref), custom_call_target="tpu_custom_call" | custom-call | tf_op jit(solution)/shard_map/pallas_call | solution.py:28
  138.4 20.8 %all-to-all-start.4 = ((f32[24,8,96]{2,1,0:T(8,128)}), f32[24,8,96]{2,1,0:T(8,128)S(1)}, u32[]{:S(2)}, u32[]{:S(2)}) async-start(f32[24,8,96]{2,1,0:T(8,128)} %shard_map.90), calls=%async_computation.4 | async-start | bytes 196608 | tf_op jit(solution)/shard_map/all_to_all | solution.py:164
  159.3 3.0 %shard_map.87 = (bf16[128,1024]{1,0:T(8,128)(2,1)}, bf16[128,1024]{1,0:T(8,128)(2,1)}) custom-call(bf16[128,1024]{1,0:T(8,128)(2,1)} %bitcast.20, bf16[128,1024]{1,0:T(8,128)(2,1)} %bitcast.23, f32[128,1024]{1,0:T(8,128)} %get-tuple-element.11.refs_2_, f32[128,1024]{1,0:T(8,128)} %get-tuple-element.12.refs_3_, f32[32,64,128]{2,1,0:T(8,128)} %copy-done), custom_call_target="tpu_custom_call" | custom-call | tf_op jit(solution)/shard_map/pallas_call | solution.py:28
  162.3 8.0 %all-to-all-done.4.in_ref = f32[24,8,96]{2,1,0:T(8,128)S(1)} async-done(((f32[24,8,96]{2,1,0:T(8,128)}), f32[24,8,96]{2,1,0:T(8,128)S(1)}, u32[]{:S(2)}, u32[]{:S(2)}) %all-to-all-start.4) | async-done | bytes 73760 | tf_op jit(solution)/shard_map/all_to_all | solution.py:164
  170.9 1.6 shard_map.91
  (27 shorter events, 5.0 us)
Async XLA Ops:
  34.0 11.5 %copy-start.7 = (bf16[1,128,1152]{2,1,0:T(8,128)(2,1)S(1)}, bf16[1,128,1152]{2,1,0:T(8,128)(2,1)}, u32[]{:S(2)}) copy-start(bf16[1,128,1152]{2,1,0:T(8,128)(2,1)} %param.9) | copy-start | bytes 884740
  36.4 56.4 %all-to-all-start.1 = ((f32[32,64,128]{2,1,0:T(8,128)}), f32[32,64,128]{2,1,0:T(8,128)S(1)}, u32[]{:S(2)}, u32[]{:S(2)}) async-start(f32[32,64,128]{2,1,0:T(8,128)} %shard_map.86), calls=%async_computation.1 | async-start | bytes 2097152 | tf_op jit(solution)/shard_map/all_to_all | solution.py:164
  45.6 55.3 %copy-start.1 = (f32[128,1152]{1,0:T(8,128)}, f32[128,1152]{1,0:T(8,128)S(1)}, u32[]{:S(2)}) copy-start(f32[128,1152]{1,0:T(8,128)S(1)} %bitcast_convert_fusion.refs_0_) | copy-start | bytes 1769476
  45.6 24.2 %collective-permute-start.1 = (f32[128,1152]{1,0:T(8,128)S(1)}, f32[128,1152]{1,0:T(8,128)S(1)}, u32[]{:S(2)}, u32[]{:S(2)}) collective-permute-start(f32[128,1152]{1,0:T(8,128)S(1)} %bitcast_convert_fusion.refs_0_), channel_id=1, source_target_pairs={{0,8},{8,16},{16,24},{24,0},{1,9},{9,17},{17,25},{25,1},{2,10},{10... | collective-permute-start | bytes 1769480 | tf_op jit(solution)/shard_map/ppermute | solution.py:172
  48.8 35.7 %collective-permute-start.3 = (f32[128,1152]{1,0:T(8,128)S(1)}, f32[128,1152]{1,0:T(8,128)S(1)}, u32[]{:S(2)}, u32[]{:S(2)}) collective-permute-start(f32[128,1152]{1,0:T(8,128)S(1)} %bitcast_convert_fusion.refs_0_), channel_id=1, source_target_pairs={{0,16},{8,24},{16,0},{24,8},{1,17},{9,25},{17,1},{25,9},{2,18},{10... | collective-permute-start | bytes 1769480 | tf_op jit(solution)/shard_map/ppermute | solution.py:172
  53.1 36.9 %collective-permute-start.5 = (f32[128,1152]{1,0:T(8,128)S(1)}, f32[128,1152]{1,0:T(8,128)S(1)}, u32[]{:S(2)}, u32[]{:S(2)}) collective-permute-start(f32[128,1152]{1,0:T(8,128)S(1)} %bitcast_convert_fusion.refs_0_), channel_id=1, source_target_pairs={{0,24},{8,0},{16,8},{24,16},{1,25},{9,1},{17,9},{25,17},{2,26},{10... | collective-permute-start | bytes 1769480 | tf_op jit(solution)/shard_map/ppermute | solution.py:172
  56.2 44.7 %collective-permute-start = (f32[128,1152]{1,0:T(8,128)S(1)}, f32[128,1152]{1,0:T(8,128)}, u32[]{:S(2)}, u32[]{:S(2)}) collective-permute-start(f32[128,1152]{1,0:T(8,128)S(1)} %bitcast_convert_fusion.refs_0_), channel_id=1, source_target_pairs={{0,32},{32,0},{1,33},{33,1},{2,34},{34,2},{3,35},{35,3},{4,36},{36... | collective-permute-start | bytes 1769480 | tf_op jit(solution)/shard_map/ppermute | solution.py:170
  69.9 31.0 %copy-start.3 = (f32[128,1152]{1,0:T(8,128)}, f32[128,1152]{1,0:T(8,128)S(1)}, u32[]{:S(2)}) copy-start(f32[128,1152]{1,0:T(8,128)S(1)} %collective-permute-done.1.refs_2_) | copy-start | bytes 1769476
  69.9 31.0 %collective-permute-start.2 = (f32[128,1152]{1,0:T(8,128)S(1)}, f32[128,1152]{1,0:T(8,128)}, u32[]{:S(2)}, u32[]{:S(2)}) collective-permute-start(f32[128,1152]{1,0:T(8,128)S(1)} %collective-permute-done.1.refs_2_), channel_id=1, source_target_pairs={{0,32},{32,0},{1,33},{33,1},{2,34},{34,2},{3,35},{35,3},{4,36},{36... | collective-permute-start | bytes 1769480 | tf_op jit(solution)/shard_map/ppermute | solution.py:173
  84.5 16.5 %copy-start.4 = (f32[128,1152]{1,0:T(8,128)}, f32[128,1152]{1,0:T(8,128)S(1)}, u32[]{:S(2)}) copy-start(f32[128,1152]{1,0:T(8,128)S(1)} %collective-permute-done.3.refs_4_) | copy-start | bytes 1769476
  84.5 16.4 %collective-permute-start.4 = (f32[128,1152]{1,0:T(8,128)S(1)}, f32[128,1152]{1,0:T(8,128)}, u32[]{:S(2)}, u32[]{:S(2)}) collective-permute-start(f32[128,1152]{1,0:T(8,128)S(1)} %collective-permute-done.3.refs_4_), channel_id=1, source_target_pairs={{0,32},{32,0},{1,33},{33,1},{2,34},{34,2},{3,35},{35,3},{4,36},{36... | collective-permute-start | bytes 1769480 | tf_op jit(solution)/shard_map/ppermute | solution.py:173
  90.1 10.8 %copy-start.5 = (f32[128,1152]{1,0:T(8,128)}, f32[128,1152]{1,0:T(8,128)S(1)}, u32[]{:S(2)}) copy-start(f32[128,1152]{1,0:T(8,128)S(1)} %collective-permute-done.5.refs_6_) | copy-start | bytes 1769476
  90.1 10.8 %collective-permute-start.6 = (f32[128,1152]{1,0:T(8,128)S(1)}, f32[128,1152]{1,0:T(8,128)}, u32[]{:S(2)}, u32[]{:S(2)}) collective-permute-start(f32[128,1152]{1,0:T(8,128)S(1)} %collective-permute-done.5.refs_6_), channel_id=1, source_target_pairs={{0,32},{32,0},{1,33},{33,1},{2,34},{34,2},{3,35},{35,3},{4,36},{36... | collective-permute-start | bytes 1769480 | tf_op jit(solution)/shard_map/ppermute | solution.py:173
  92.8 1.0 copy-start
  96.4 13.3 %all-to-all-start.2 = ((f32[8,128,128]{2,1,0:T(8,128)}), f32[8,128,128]{2,1,0:T(8,128)S(1)}, u32[]{:S(2)}, u32[]{:S(2)}) async-start(f32[8,128,128]{2,1,0:T(8,128)} %get-tuple-element.17), calls=%async_computation.2 | async-start | bytes 1048576 | tf_op jit(solution)/shard_map/all_to_all | solution.py:164
  109.7 0.8 copy-start.2
  138.4 31.9 %all-to-all-start.4 = ((f32[24,8,96]{2,1,0:T(8,128)}), f32[24,8,96]{2,1,0:T(8,128)S(1)}, u32[]{:S(2)}, u32[]{:S(2)}) async-start(f32[24,8,96]{2,1,0:T(8,128)} %shard_map.90), calls=%async_computation.4 | async-start | bytes 196608 | tf_op jit(solution)/shard_map/all_to_all | solution.py:164
  170.3 0.6 copy-start.6
